TPU v7x, 32 devices: a whole 2x2x4 slice. The times are simulated.
32 devices in a mesh: grid: 8 (over y, x, core), sub: 4 (over z).
Axes of the slice: x: 2, y: 2, z: 4, core: 2. Of those that a mesh axis runs over, the one named last changes fastest.
Arguments:
- grid_x: bfloat16 [65536, 512], P(('grid', 'sub')), may hold values from -6 to 6
- mesh_h: bfloat16 [2048, 512], P(('grid', 'sub')), may hold values from -6 to 6
- gain_grid: float32 [512], replicated, may hold values from 0.1 to 1.9
- gain_mesh: float32 [512], replicated, may hold values from 0.1 to 1.9
- w_query: bfloat16 [512, 512], replicated, may hold values from -0.25 to 0.25
- w_key: bfloat16 [512, 512], replicated, may hold values from -0.25 to 0.25
- w_value: bfloat16 [512, 512], replicated, may hold values from -0.25 to 0.25
- w_out: bfloat16 [512, 512], replicated, may hold values from -0.25 to 0.25
- edge_bias: float32 [2048, 384], P(('grid', 'sub')), may hold values from -9 to 300
- neighbours: int32 [2048, 96], P(('grid', 'sub')), may hold values from 0 to 767, as said below
- valid: int32 [2048, 96], P(('grid', 'sub')), may hold values from 0 to 1, as said below
- send_rows: int32 [32, 3, 4, 64], P(('grid', 'sub')), may hold values from 0 to 2047, as said below
- out_grad: bfloat16 [2048, 512], P(('grid', 'sub')), may hold values from -24 to 24
Outputs:
- mesh_out: bfloat16 [2048, 512], P(('grid', 'sub'))
- mesh_grad: bfloat16 [2048, 512], P(('grid', 'sub'))
- grid_grad: bfloat16 [65536, 512], P(('grid', 'sub'))
- weight_grads: float32 [4, 512, 512], replicated
Inputs may be any that keep to these rules, and one draw needn't show every extreme that they name: `send_rows`: for each source device, slab offset and destination sub index the 64 local rows are distinct; rows sent to the slab below (o = 0) lie in the lower half of the device's 2048 rows, rows sent to the slab above (o = 2) in the upper half. `neighbours`: a slot (o * 4 + s) * 64 + t names row t of what device s of slab g - o + 1 sends to the node's device; slots of slabs outside the grid are never named; the 96 entries of a node are distinct; some slots are named by no node. The first two edges of every node are valid.
All inputs are finite; a program needn't handle non-finite values.
Results may differ from a plain program's by a relative error of at most 0.009.
Values may be sent and summed in bfloat16 or wider, within the bound.
A program may use at most 128 MiB of HBM per device.

v0:
```python
import jax
import jax.numpy as jnp
from jax import lax
from jax.sharding import PartitionSpec as P

EPSILON = 1e-06
NEG_FILL = -1e30


def from_behind(block, axis, distance):
    devices = range(lax.axis_size(axis))
    route = [(i - distance, i) for i in devices if i - distance in devices]
    return lax.ppermute(block, axis, route)


def normalize(values_in, gain_row):
    widened = values_in.astype(jnp.float32)
    factor = lax.rsqrt(jnp.mean(widened * widened, axis=-1, keepdims=True) + EPSILON)
    return (widened, factor, (widened * factor * gain_row).astype(jnp.bfloat16))


def normalize_back(widened, factor, gain_row, upstream):
    scaled = gain_row * upstream
    inner_mean = jnp.mean(widened * scaled, axis=-1, keepdims=True)
    return factor * scaled - widened * factor**3 * inner_mean


def shards(
    grid_x,
    mesh_h,
    gain_grid,
    gain_mesh,
    w_query,
    w_key,
    w_value,
    w_out,
    edge_bias,
    neighbours,
    valid,
    send_rows,
    out_grad,
):
    point_count, model_width = grid_x.shape
    node_count = mesh_h.shape[0]
    sub_count = send_rows.shape[2]
    slots_per = send_rows.shape[3]
    block = sub_count * slots_per
    slot_count = 3 * block
    fanout = neighbours.shape[1]
    head_count = edge_bias.shape[1] // fanout
    head_width = model_width // head_count
    logit_scale = head_width ** (-0.5)
    w_pair = jnp.concatenate([w_key, w_value], axis=1)
    grid_wide, grid_factor, grid_normed = normalize(grid_x, gain_grid)
    flat_rows = send_rows[0].reshape(slot_count)
    send_match = flat_rows[:, None] == jnp.arange(point_count, dtype=jnp.int32)[None, :]
    send_onehot = send_match.astype(jnp.bfloat16)
    sent_normed = jnp.dot(send_onehot, grid_normed, preferred_element_type=jnp.float32).astype(
        jnp.bfloat16
    )
    packet = sent_normed.reshape(3, sub_count, slots_per, model_width)
    packet_width = packet.shape[3]
    mixed = lax.all_to_all(packet, "sub", split_axis=1, concat_axis=1, tiled=True).reshape(
        3, block, packet_width
    )
    pieces = []
    for offset in (0, 1, 2):
        piece = mixed[offset]
        if offset != 1:
            piece = from_behind(piece, "grid", offset - 1)
        pieces.append(piece)
    arrived = jnp.concatenate(pieces, axis=0)
    recv_pair = jnp.dot(arrived, w_pair, preferred_element_type=jnp.float32).astype(jnp.bfloat16)
    slot_onehot = (
        neighbours[:, :, None] == jnp.arange(slot_count, dtype=jnp.int32)[None, None, :]
    ).astype(jnp.bfloat16)
    edge_pair = jnp.einsum(
        "gjc,ce->gje", slot_onehot, recv_pair, preferred_element_type=jnp.float32
    ).astype(jnp.bfloat16)
    edge_keys = edge_pair[:, :, :model_width].reshape(node_count, fanout, head_count, head_width)
    edge_values = edge_pair[:, :, model_width:].reshape(node_count, fanout, head_count, head_width)
    mesh_wide, mesh_factor, mesh_normed = normalize(mesh_h, gain_mesh)
    queries = (
        jnp.dot(mesh_normed, w_query, preferred_element_type=jnp.float32) * logit_scale
    ).astype(jnp.bfloat16)
    query_head_rows = queries.reshape(node_count, head_count, head_width)
    score_matrix = jnp.einsum(
        "gip,gjip->gij", query_head_rows, edge_keys, preferred_element_type=jnp.float32
    ) + edge_bias.reshape(node_count, head_count, fanout)
    live_mask = (valid == 1)[:, None, :]
    row_peak = jnp.max(jnp.where(live_mask, score_matrix, NEG_FILL), axis=2, keepdims=True)
    exp_terms = jnp.exp(jnp.where(live_mask, score_matrix - row_peak, NEG_FILL))
    attn_probs = exp_terms / jnp.sum(exp_terms, axis=2, keepdims=True)
    probabilities_batch = attn_probs.astype(jnp.bfloat16)
    attended_rows = (
        jnp.einsum(
            "gij,gjik->gik", probabilities_batch, edge_values, preferred_element_type=jnp.float32
        )
        .reshape(node_count, model_width)
        .astype(jnp.bfloat16)
    )
    mesh_out = (
        mesh_wide + jnp.dot(attended_rows, w_out, preferred_element_type=jnp.float32)
    ).astype(jnp.bfloat16)
    grad_wo = jnp.einsum("md,me->de", attended_rows, out_grad, preferred_element_type=jnp.float32)
    att_grad = jnp.einsum("me,de->md", out_grad, w_out, preferred_element_type=jnp.float32).astype(
        jnp.bfloat16
    )
    head_gradient = att_grad.reshape(node_count, head_count, head_width)
    probability_gradient = jnp.einsum(
        "gip,gjip->gij", head_gradient, edge_values, preferred_element_type=jnp.float32
    )
    score_gradient = (
        attn_probs
        * (probability_gradient - jnp.sum(attn_probs * probability_gradient, axis=2, keepdims=True))
    ).astype(jnp.bfloat16)
    query_gradient = (
        (
            jnp.einsum(
                "gij,gjik->gik", score_gradient, edge_keys, preferred_element_type=jnp.float32
            )
            * logit_scale
        )
        .reshape(node_count, model_width)
        .astype(jnp.bfloat16)
    )
    dense_score_gradient = jnp.einsum(
        "gij,gjc->gic", score_gradient, slot_onehot, preferred_element_type=jnp.float32
    ).astype(jnp.bfloat16)
    dense_probabilities = jnp.einsum(
        "gij,gjc->gic", probabilities_batch, slot_onehot, preferred_element_type=jnp.float32
    ).astype(jnp.bfloat16)
    key_part = jnp.einsum(
        "uza,uzt->azt", dense_score_gradient, query_head_rows, preferred_element_type=jnp.float32
    ).reshape(slot_count, model_width)
    value_part = jnp.einsum(
        "uza,uzt->azt", dense_probabilities, head_gradient, preferred_element_type=jnp.float32
    ).reshape(slot_count, model_width)
    back_packet = (
        jnp.concatenate([key_part, value_part], axis=1)
        .astype(jnp.bfloat16)
        .reshape(3, block, 2 * model_width)
    )
    home_pieces = []
    for offset in (0, 1, 2):
        piece = back_packet[offset]
        if offset != 1:
            piece = from_behind(piece, "grid", 1 - offset)
        home_pieces.append(piece)
    home = jnp.stack(home_pieces)
    home = home.reshape(3, sub_count, slots_per, 2 * model_width)
    returned = lax.all_to_all(home, "sub", split_axis=1, concat_axis=1, tiled=True).reshape(
        slot_count, 2 * model_width
    )
    pair_grads = jnp.einsum("sd,se->de", sent_normed, returned, preferred_element_type=jnp.float32)
    slot_back = jnp.einsum("se,de->sd", returned, w_pair, preferred_element_type=jnp.float32)
    normed_grad = jnp.einsum(
        "sp,sd->pd",
        send_match.astype(jnp.float32),
        slot_back,
        precision=lax.Precision.HIGHEST,
        preferred_element_type=jnp.float32,
    )
    grid_grad = normalize_back(grid_wide, grid_factor, gain_grid, normed_grad).astype(jnp.bfloat16)
    grad_wq = jnp.einsum(
        "md,me->de", mesh_normed, query_gradient, preferred_element_type=jnp.float32
    )
    mesh_normed_grad = jnp.einsum(
        "me,de->md", query_gradient, w_query, preferred_element_type=jnp.float32
    )
    mesh_grad = (
        out_grad.astype(jnp.float32)
        + normalize_back(mesh_wide, mesh_factor, gain_mesh, mesh_normed_grad)
    ).astype(jnp.bfloat16)
    local_grads = jnp.stack(
        [grad_wq, pair_grads[:, :model_width], pair_grads[:, model_width:], grad_wo]
    )
    weight_grads = lax.psum(local_grads, ("grid", "sub"))
    return (mesh_out, mesh_grad, grid_grad, weight_grads)


def solution(mesh):
    in_specs = (
        P(("grid", "sub"), None),
        P(("grid", "sub"), None),
        P(),
        P(),
        P(),
        P(),
        P(),
        P(),
        P(("grid", "sub"), None),
        P(("grid", "sub"), None),
        P(("grid", "sub"), None),
        P(("grid", "sub"), None, None, None),
        P(("grid", "sub"), None),
    )
    out_specs = (P(("grid", "sub"), None), P(("grid", "sub"), None), P(("grid", "sub"), None), P())
    return jax.shard_map(shards, mesh=mesh, in_specs=in_specs, out_specs=out_specs, check_vma=False)
```

profile of v0, /device:TPU:0, one launch (start us, length us, event | category | flops | bytes accessed | tf_op | source)
XLA Modules:
  0.0 303.4 jit_solution(8482572767754308976)
XLA Ops:
  7.2 3.0 copy.27
  10.8 2.0 fusion.35
  14.6 6.3 %all-to-all-start = ((bf16[3,4,64,512]{3,2,0,1:T(8,128)(2,1)}), bf16[3,4,64,512]{3,2,0,1:T(8,128)(2,1)S(1)}, u32[]{:S(2)}, u32[]{:S(2)}) async-start(bf16[3,4,64,512]{3,2,0,1:T(8,128)(2,1)} %copy.28), calls=%async_computation | async-start | bytes 1572864 | tf_op jit(solution)/shard_map/all_to_all | solution.py:63
  24.1 17.0 %all-to-all-done = bf16[3,4,64,512]{3,2,0,1:T(8,128)(2,1)S(1)} async-done(((bf16[3,4,64,512]{3,2,0,1:T(8,128)(2,1)}), bf16[3,4,64,512]{3,2,0,1:T(8,128)(2,1)S(1)}, u32[]{:S(2)}, u32[]{:S(2)}) %all-to-all-start) | async-done | bytes 786464 | tf_op jit(solution)/shard_map/all_to_all | solution.py:63
  42.4 3.2 %collective-permute-start.1 = (bf16[256,512]{1,0:T(8,128)(2,1)S(1)}, bf16[256,512]{1,0:T(8,128)(2,1)S(1)}, u32[]{:S(2)}, u32[]{:S(2)}) collective-permute-start(bf16[256,512]{1,0:T(8,128)(2,1)S(1)} %bitcast.119), channel_id=1, source_target_pairs={{0,4},{4,8},{8,12},{12,16},{16,20},{20,24},{24,28},{1,5},{5,9},{9,... | collective-permute-start | bytes 786440 | tf_op jit(solution)/shard_map/ppermute | solution.py:13
  46.8 2.2 fusion.123
  49.0 11.4 %fusion.7 = bf16[64,96,1024]{2,1,0:T(8,128)(2,1)S(1)} fusion(s32[64,96]{1,0:T(8,128)} %param.22, bf16[768,1024,1]{1,0,2:T(8,128)(2,1)S(1)} %fusion.123), kind=kOutput, calls=%fused_computation.12 | convolution fusion | flops 9674686464 | bytes 14180352 | tf_op jit(solution)/shard_map/gjc,ce->gje/dot_general | solution.py:77
  60.5 3.7 %slice_bitcast_fusion.1 = (bf16[64,12,4,8,128]{4,3,2,1,0:T(8,128)(2,1)S(1)}, bf16[64,12,4,8,128]{4,3,2,1,0:T(8,128)(2,1)S(1)}) fusion(bf16[64,96,1024]{2,1,0:T(8,128)(2,1)S(1)} %fusion.7), kind=kLoop, calls=%fused_computation.22 | loop fusion | bytes 25165824
  64.2 3.3 %fusion.14 = f32[64,4,1,96]{3,2,1,0:T(1,128)S(1)} fusion(bf16[64,4,128,1]{2,3,1,0:T(2,128)(2,1)S(1)} %reshape.124, bf16[64,12,4,8,128]{4,3,2,1,0:T(8,128)(2,1)S(1)} %get-tuple-element.16), kind=kOutput, calls=%fused_computation.19 | convolution fusion | flops 6291456 | bytes 6455296 | tf_op jit(solution)/shard_map/gip,gjip->gij/dot_general | solution.py:87
  67.6 3.3 %fusion.8 = f32[64,4,1,96]{3,2,1,0:T(1,128)S(1)} fusion(bf16[64,4,128,1]{2,3,1,0:T(2,128)(2,1)S(1)} %reshape.126, bf16[64,12,4,8,128]{4,3,2,1,0:T(8,128)(2,1)S(1)} %get-tuple-element.17), kind=kOutput, calls=%fused_computation.13 | convolution fusion | flops 6291456 | bytes 6455296 | tf_op jit(solution)/shard_map/gip,gjip->gij/dot_general | solution.py:110
  71.2 3.6 %fusion.39 = bf16[64,4,768]{2,1,0:T(4,128)(2,1)S(1)} fusion(s32[64,96]{1,0:T(8,128)S(1)} %copy-done.29, f32[64,4,96]{2,1,0:T(4,128)S(1)} %get-tuple-element.33, f32[64,4]{1,0:T(8,128)S(1)} %get-tuple-element.32), kind=kOutput, calls=%fused_computation.55 | convolution fusion | flops 42713088 | bytes 517120 | tf_op jit(solution)/shard_map/gij,gjc->gic/dot_general | solution.py:130
  75.8 3.5 %fusion.38 = bf16[64,4,768]{2,1,0:T(4,128)(2,1)S(1)} fusion(bf16[64,4,96]{2,1,0:T(4,128)(2,1)S(1)} %get-tuple-element.26, s32[64,96]{1,0:T(8,128)S(1)} %copy-done.29), kind=kOutput, calls=%fused_computation.54 | convolution fusion | flops 42663936 | bytes 466944 | tf_op jit(solution)/shard_map/gij,gjc->gic/dot_general | solution.py:127
  81.0 5.0 %collective-permute-start.2 = (bf16[256,1024]{1,0:T(8,128)(2,1)S(1)}, bf16[256,1024]{1,0:T(8,128)(2,1)S(1)}, u32[]{:S(2)}, u32[]{:S(2)}) collective-permute-start(bf16[256,1024]{1,0:T(8,128)(2,1)S(1)} %get-tuple-element.20), channel_id=1, source_target_pairs={{0,4},{4,8},{8,12},{12,16},{16,20},{20,24},{24,28},{1,5},{5,9},{9,... | collective-permute-start | bytes 1572872 | tf_op jit(solution)/shard_map/ppermute | solution.py:13
  87.5 4.3 %collective-permute-done.3 = bf16[256,1024]{1,0:T(8,128)(2,1)S(1)} collective-permute-done((bf16[256,1024]{1,0:T(8,128)(2,1)S(1)}, bf16[256,1024]{1,0:T(8,128)(2,1)S(1)}, u32[]{:S(2)}, u32[]{:S(2)}) %collective-permute-start.3) | collective-permute-done | bytes 524320 | tf_op jit(solution)/shard_map/ppermute | solution.py:13
  93.2 4.4 %all-to-all-start.1 = ((bf16[3,4,64,1024]{3,2,0,1:T(8,128)(2,1)}), bf16[3,4,64,1024]{3,2,0,1:T(8,128)(2,1)}, u32[]{:S(2)}, u32[]{:S(2)}) async-start(bf16[3,4,64,1024]{3,2,0,1:T(8,128)(2,1)} %copy.35), calls=%async_computation.1 | async-start | bytes 3145728 | tf_op jit(solution)/shard_map/all_to_all | solution.py:152
  97.9 4.7 %fusion.10 = f32[64,4,1,128]{3,2,1,0:T(1,128)S(1)} fusion(bf16[64,12,4,8,128]{4,3,2,1,0:T(8,128)(2,1)} %copy-done.2, bf16[64,4,96,1]{2,1,0,3:T(4,128)(2,1)S(1)} %copy-done.16), kind=kOutput, calls=%fused_computation.15 | convolution fusion | flops 6291456 | bytes 6471680 | tf_op jit(solution)/shard_map/gij,gjik->gik/dot_general | solution.py:96
  106.5 24.3 %all-to-all-done.1 = bf16[3,4,64,1024]{3,2,0,1:T(8,128)(2,1)} async-done(((bf16[3,4,64,1024]{3,2,0,1:T(8,128)(2,1)}), bf16[3,4,64,1024]{3,2,0,1:T(8,128)(2,1)}, u32[]{:S(2)}, u32[]{:S(2)}) %all-to-all-start.1) | async-done | bytes 1572896 | tf_op jit(solution)/shard_map/all_to_all | solution.py:152
  134.2 2.5 pad_maximum_fusion
  138.8 2.7 fusion.93
  141.6 6.1 %fusion.28 = (f32[2048]{0:T(1024)S(1)}, f32[2048,512]{0,1:T(8,128)S(1)}) fusion(bf16[2048,512]{0,1:T(8,128)(2,1)S(1)} %copy-done.4, f32[512]{0:T(512)S(1)} %copy-done.27, f32[768,512]{1,0:T(8,128)S(1)} %fusion.93, s32[768]{0:T(1024)S(1)} %copy-done.25), kind=kOutput, calls=%fused_computation.36 | convolution fusion | flops 9669441536 | bytes 7877632 | tf_op jit(solution)/shard_map/sp,sd->pd/dot_general | solution.py:157
  147.7 2.6 fusion.27
  150.3 3.9 %copy.37 = bf16[2048,512]{1,0:T(8,128)(2,1)} copy(bf16[2048,512]{0,1:T(8,128)(2,1)} %fusion.27) | data formatting | bytes 4194304
  154.2 137.7 %all-reduce.2.cloned.1.call-done = f32[4,512,512]{2,1,0:T(8,128)} async-done(((f32[4,512,512]{2,1,0:T(8,128)}), f32[4,512,512]{2,1,0:T(8,128)}) %all-reduce.2.cloned.1.call-update) | async-done | bytes 4194320 | tf_op jit(solution)/shard_map/psum | solution.py:178
  291.9 4.6 %copy.106 = f32[4,512,512]{2,1,0:T(8,128)} copy(f32[4,512,512]{2,1,0:T(8,128)} %all-reduce.2.cloned.1.call-done) | data formatting | bytes 8388608
  (110 shorter events, 23.4 us)
Async XLA Ops:
  7.2 16.6 %copy-start = (bf16[512,512]{1,0:T(8,128)(2,1)S(1)}, bf16[512,512]{1,0:T(8,128)(2,1)}, u32[]{:S(2)}) copy-start(bf16[512,512]{1,0:T(8,128)(2,1)} %param.17) | copy-start | bytes 1572868
  10.8 10.2 %copy-start.6 = (bf16[64,512]{1,0:T(8,128)(2,1)S(1)}, bf16[64,512]{1,0:T(8,128)(2,1)}, u32[]{:S(2)}) copy-start(bf16[64,512]{1,0:T(8,128)(2,1)} %param.14) | copy-start | bytes 196612
  12.8 10.7 %copy-start.7 = (bf16[512,512]{1,0:T(8,128)(2,1)S(1)}, bf16[512,512]{1,0:T(8,128)(2,1)}, u32[]{:S(2)}) copy-start(bf16[512,512]{1,0:T(8,128)(2,1)} %param.20) | copy-start | bytes 1572868
  12.8 10.7 %copy-start.11 = (bf16[64,512]{1,0:T(8,128)(2,1)S(1)}, bf16[64,512]{1,0:T(8,128)(2,1)}, u32[]{:S(2)}) copy-start(bf16[64,512]{1,0:T(8,128)(2,1)} %param.25) | copy-start | bytes 196612
  13.7 10.1 %copy-start.18 = (f32[512]{0:T(512)S(1)}, f32[512]{0:T(512)}, u32[]{:S(2)}) copy-start(f32[512]{0:T(512)} %param.16) | copy-start | bytes 6148
  13.7 32.0 %copy-start.12 = (bf16[512,512]{1,0:T(8,128)(2,1)S(1)}, bf16[512,512]{1,0:T(8,128)(2,1)}, u32[]{:S(2)}) copy-start(bf16[512,512]{1,0:T(8,128)(2,1)} %param.19) | copy-start | bytes 1572868
  13.7 32.9 %copy-start.13 = (f32[64,384]{1,0:T(8,128)S(1)}, f32[64,384]{1,0:T(8,128)}, u32[]{:S(2)}) copy-start(f32[64,384]{1,0:T(8,128)} %param.21) | copy-start | bytes 294916
  13.7 33.1 %copy-start.17 = (s32[64,96]{1,0:T(8,128)S(1)}, s32[64,96]{1,0:T(8,128)}, u32[]{:S(2)}) copy-start(s32[64,96]{1,0:T(8,128)} %param.23) | copy-start | bytes 73732
  14.6 26.5 %all-to-all-start = ((bf16[3,4,64,512]{3,2,0,1:T(8,128)(2,1)}), bf16[3,4,64,512]{3,2,0,1:T(8,128)(2,1)S(1)}, u32[]{:S(2)}, u32[]{:S(2)}) async-start(bf16[3,4,64,512]{3,2,0,1:T(8,128)(2,1)} %copy.28), calls=%async_computation | async-start | bytes 1572864 | tf_op jit(solution)/shard_map/all_to_all | solution.py:63
  41.1 5.7 %collective-permute-start = (bf16[256,512]{1,0:T(8,128)(2,1)S(1)}, bf16[256,512]{1,0:T(8,128)(2,1)S(1)}, u32[]{:S(2)}, u32[]{:S(2)}) collective-permute-start(bf16[256,512]{1,0:T(8,128)(2,1)S(1)} %bitcast.120), channel_id=1, source_target_pairs={{4,0},{8,4},{12,8},{16,12},{20,16},{24,20},{28,24},{5,1},{9,5},{13... | collective-permute-start | bytes 786440 | tf_op jit(solution)/shard_map/ppermute | solution.py:13
  42.4 4.4 %collective-permute-start.1 = (bf16[256,512]{1,0:T(8,128)(2,1)S(1)}, bf16[256,512]{1,0:T(8,128)(2,1)S(1)}, u32[]{:S(2)}, u32[]{:S(2)}) collective-permute-start(bf16[256,512]{1,0:T(8,128)(2,1)S(1)} %bitcast.119), channel_id=1, source_target_pairs={{0,4},{4,8},{8,12},{12,16},{16,20},{20,24},{24,28},{1,5},{5,9},{9,... | collective-permute-start | bytes 786440 | tf_op jit(solution)/shard_map/ppermute | solution.py:13
  64.2 6.7 %copy-start.1 = (bf16[64,12,4,8,128]{4,3,2,1,0:T(8,128)(2,1)}, bf16[64,12,4,8,128]{4,3,2,1,0:T(8,128)(2,1)S(1)}, u32[]{:S(2)}) copy-start(bf16[64,12,4,8,128]{4,3,2,1,0:T(8,128)(2,1)S(1)} %get-tuple-element.16) | copy-start | bytes 18874372
  64.2 6.7 %copy-start.2 = (bf16[64,12,4,8,128]{4,3,2,1,0:T(8,128)(2,1)}, bf16[64,12,4,8,128]{4,3,2,1,0:T(8,128)(2,1)S(1)}, u32[]{:S(2)}) copy-start(bf16[64,12,4,8,128]{4,3,2,1,0:T(8,128)(2,1)S(1)} %get-tuple-element.17) | copy-start | bytes 18874372
  81.0 6.5 %collective-permute-start.2 = (bf16[256,1024]{1,0:T(8,128)(2,1)S(1)}, bf16[256,1024]{1,0:T(8,128)(2,1)S(1)}, u32[]{:S(2)}, u32[]{:S(2)}) collective-permute-start(bf16[256,1024]{1,0:T(8,128)(2,1)S(1)} %get-tuple-element.20), channel_id=1, source_target_pairs={{0,4},{4,8},{8,12},{12,16},{16,20},{20,24},{24,28},{1,5},{5,9},{9,... | collective-permute-start | bytes 1572872 | tf_op jit(solution)/shard_map/ppermute | solution.py:13
  86.0 5.8 %collective-permute-start.3 = (bf16[256,1024]{1,0:T(8,128)(2,1)S(1)}, bf16[256,1024]{1,0:T(8,128)(2,1)S(1)}, u32[]{:S(2)}, u32[]{:S(2)}) collective-permute-start(bf16[256,1024]{1,0:T(8,128)(2,1)S(1)} %get-tuple-element.21), channel_id=1, source_target_pairs={{4,0},{8,4},{12,8},{16,12},{20,16},{24,20},{28,24},{5,1},{9,5},{13... | collective-permute-start | bytes 1572872 | tf_op jit(solution)/shard_map/ppermute | solution.py:13
  91.7 6.1 %copy-start.16 = (bf16[64,4,96,1]{2,1,0,3:T(4,128)(2,1)S(1)}, bf16[64,4,96,1]{2,1,0,3:T(4,128)(2,1)}, u32[]{:S(2)}) copy-start(bf16[64,4,96,1]{2,1,0,3:T(4,128)(2,1)} %get-tuple-element.27) | copy-start | bytes 147460
  91.9 12.0 %slice-start = ((s8[6291456]{0:T(1024)(128)(4,1)}), s8[2097152]{0:T(1024)(128)(4,1)S(1)}, s32[]{:S(2)}) async-start(s8[6291456]{0:T(1024)(128)(4,1)} %bitcast.102), calls=%async_computation.3 | async-start | bytes 4194304
  93.2 37.6 %all-to-all-start.1 = ((bf16[3,4,64,1024]{3,2,0,1:T(8,128)(2,1)}), bf16[3,4,64,1024]{3,2,0,1:T(8,128)(2,1)}, u32[]{:S(2)}, u32[]{:S(2)}) async-start(bf16[3,4,64,1024]{3,2,0,1:T(8,128)(2,1)} %copy.35), calls=%async_computation.1 | async-start | bytes 3145728 | tf_op jit(solution)/shard_map/all_to_all | solution.py:152
  97.6 194.4 %all-reduce.2.cloned.1.call-start = ((), (), s32[]{:S(2)}) async-start(), calls=%async_computation.2 | async-start | bytes 8388608 | tf_op jit(solution)/shard_map/psum | solution.py:178
  97.8 6.0 %copy-start.15 = (bf16[64,4,96]{2,1,0:T(4,128)(2,1)S(1)}, bf16[64,4,96]{2,1,0:T(4,128)(2,1)}, u32[]{:S(2)}) copy-start(bf16[64,4,96]{2,1,0:T(4,128)(2,1)} %copy-done.14) | copy-start | bytes 147460
  97.9 6.0 %slice-start.1 = ((s8[6291456]{0:T(1024)(128)(4,1)}), s8[4194304]{0:T(1024)(128)(4,1)S(1)}, s32[]{:S(2)}) async-start(s8[6291456]{0:T(1024)(128)(4,1)} %bitcast.102), calls=%async_computation.4 | async-start | bytes 8388608
  105.6 26.8 %copy-start.10 = (bf16[768,512]{1,0:T(8,128)(2,1)S(1)}, bf16[768,512]{1,0:T(8,128)(2,1)}, u32[]{:S(2)}) copy-start(bf16[768,512]{1,0:T(8,128)(2,1)} %copy-done.9) | copy-start | bytes 2359300
  136.6 4.9 %copy-start.25 = (s32[768]{0:T(1024)S(1)}, s32[768]{0:T(1024)}, u32[]{:S(2)}) copy-start(s32[768]{0:T(1024)} %copy-done.24) | copy-start | bytes 9220
  136.6 4.9 %copy-start.27 = (f32[512]{0:T(512)S(1)}, f32[512]{0:T(512)}, u32[]{:S(2)}) copy-start(f32[512]{0:T(512)} %param.15) | copy-start | bytes 6148
  (15 other events, 36.2 us)
Sparse Core Ops, SparseCore 0:
  136.8 155.1 all-reduce.1
where the time goes:
time: 304 us; the launch traced here: 303 us
  waiting for transfers between devices  184 us (61%)
  matrix products  49.8 us (16%)
  local copies, waits for them, and re-layouts  25.1 us (8%)
  starting transfers between devices  21.8 us (7%)
  between operations  14.6 us (5%)
  other arithmetic  8.64 us (3%)
    psum x1, waiting for transfers between devices, shards(): weight_grads = lax.psum(local_grads, ('grid', 'sub'))  138 us
    all_to_all x1, waiting for transfers between devices, shards(): lax.all_to_all(home, 'sub', split_axis=1, concat_axis=1, tiled=True)  24.3 us
    unnamed x69, local copies, waits for them, and re-layouts  19.4 us
    all_to_all x1, waiting for transfers between devices, shards(): lax.all_to_all(packet, 'sub', split_axis=1, concat_axis=1, tiled=True)  17 us
    dot_general x1, matrix products, shards(): jnp.einsum('gjc,ce->gje', slot_onehot, recv_pair, preferred_element_type=...  11.4 us
    ppermute x4, starting transfers between devices, from_behind(): return lax.ppermute(block, axis, route)  10.8 us
    all_to_all x1, starting transfers between devices, shards(): lax.all_to_all(packet, 'sub', split_axis=1, concat_axis=1, tiled=True)  6.35 us
    dot_general x1, matrix products, shards(): jnp.einsum('sp,sd->pd', send_match.astype(jnp.float32), slot_back, precis...  6.08 us
  transfers between devices with their start and end apart: 7, of which 5 were waited for; matrix products, arithmetic and copies ran while one was open for 10% of the time, Pallas kernels for 0%

commit v1 on v0

v1 whole, which is shorter than its diff:
```python
import functools

import jax
import jax.numpy as jnp
from jax import lax
from jax.experimental import pallas as pl
from jax.sharding import PartitionSpec as P

EPSILON = 1e-06
NEG_FILL = -1e30


def from_behind(block, axis, distance):
    devices = range(lax.axis_size(axis))
    route = [(i - distance, i) for i in devices if i - distance in devices]
    return lax.ppermute(block, axis, route)


def normalize(values_in, gain_row):
    widened = values_in.astype(jnp.float32)
    factor = lax.rsqrt(jnp.mean(widened * widened, axis=-1, keepdims=True) + EPSILON)
    return (widened, factor, (widened * factor * gain_row).astype(jnp.bfloat16))


def normalize_back(widened, factor, gain_row, upstream):
    scaled = gain_row * upstream
    inner_mean = jnp.mean(widened * scaled, axis=-1, keepdims=True)
    return factor * scaled - widened * factor**3 * inner_mean


def spread_edges(nbr_ref, rows_ref, out_ref):
    slots = out_ref.shape[2]
    fanout = nbr_ref.shape[1]
    slot_ids = lax.broadcasted_iota(jnp.int32, (slots, fanout), 0)
    for node in range(nbr_ref.shape[0]):
        names = slot_ids == nbr_ref[pl.ds(node, 1), :]
        onehot = jnp.where(names, 1.0, 0.0).astype(jnp.bfloat16)
        spread = lax.dot_general(
            rows_ref[node], onehot, (((1,), (1,)), ((), ())), preferred_element_type=jnp.float32
        )
        out_ref[node] = (spread[16:24] + spread[8:16]) + spread[:8]


def attend(scale, q_ref, k_ref, v_ref, ag_ref, bias_ref, live_ref, att_ref, qg_ref, back_ref):
    queries, keys, values, att_grad = q_ref[...], k_ref[...], v_ref[...], ag_ref[...]
    nt = (((1,), (1,)), ((), ()))
    tn = (((0,), (0,)), ((), ()))

    def dot(a, b, dims):
        return lax.dot_general(a, b, dims, preferred_element_type=jnp.float32)

    live = live_ref[0] > 0.5
    scores = dot(queries, keys, nt) + bias_ref[0]
    peak = jnp.max(jnp.where(live, scores, NEG_FILL), axis=1, keepdims=True)
    terms = jnp.exp(jnp.where(live, scores - peak, NEG_FILL))
    probs = terms / jnp.sum(terms, axis=1, keepdims=True)
    probs_b = probs.astype(jnp.bfloat16)
    nn = (((1,), (0,)), ((), ()))
    att_ref[...] = dot(probs_b, values, nn).astype(jnp.bfloat16)
    prob_grads = dot(att_grad, values, nt)
    score_grads = (
        probs * (prob_grads - jnp.sum(probs * prob_grads, axis=1, keepdims=True))
    ).astype(jnp.bfloat16)
    qg_ref[...] = (dot(score_grads, keys, nn) * scale).astype(jnp.bfloat16)
    back_ref[0] = dot(score_grads, queries, tn).astype(jnp.bfloat16)
    back_ref[1] = dot(probs_b, att_grad, tn).astype(jnp.bfloat16)


def reduce_weights(local_grads):
    return lax.psum(local_grads, ("grid", "sub"))


def shards(
    grid_x,
    mesh_h,
    gain_grid,
    gain_mesh,
    w_query,
    w_key,
    w_value,
    w_out,
    edge_bias,
    neighbours,
    valid,
    send_rows,
    out_grad,
):
    point_count, model_width = grid_x.shape
    node_count = mesh_h.shape[0]
    sub_count = send_rows.shape[2]
    slots_per = send_rows.shape[3]
    block = sub_count * slots_per
    slot_count = 3 * block
    fanout = neighbours.shape[1]
    head_count = edge_bias.shape[1] // fanout
    head_width = model_width // head_count
    logit_scale = head_width ** (-0.5)
    w_pair = jnp.concatenate([w_key, w_value], axis=1)
    grid_wide, grid_factor, grid_normed = normalize(grid_x, gain_grid)
    flat_rows = send_rows[0].reshape(slot_count)
    send_match = flat_rows[:, None] == jnp.arange(point_count, dtype=jnp.int32)[None, :]
    send_onehot = send_match.astype(jnp.bfloat16)
    sent_normed = jnp.dot(send_onehot, grid_normed, preferred_element_type=jnp.float32).astype(
        jnp.bfloat16
    )
    packet = sent_normed.reshape(3, sub_count, slots_per, model_width)
    packet_width = packet.shape[3]
    mixed = lax.all_to_all(packet, "sub", split_axis=1, concat_axis=1, tiled=True).reshape(
        3, block, packet_width
    )
    pieces = []
    for offset in (0, 1, 2):
        piece = mixed[offset]
        if offset != 1:
            piece = from_behind(piece, "grid", offset - 1)
        pieces.append(piece)
    arrived = jnp.concatenate(pieces, axis=0)
    recv_pair = jnp.dot(arrived, w_pair, preferred_element_type=jnp.float32).astype(jnp.bfloat16)
    bias = edge_bias.reshape(node_count, head_count, fanout)
    high = lax.reduce_precision(bias, 8, 7)
    middle = lax.reduce_precision(bias - high, 8, 7)
    low = bias - high - middle
    live_row = (valid == 1).astype(jnp.float32)[:, None, :]
    filler = jnp.zeros((node_count, 8 - head_count, fanout), jnp.float32)
    live_fill = jnp.concatenate([live_row, filler[:, 1:]], axis=1)
    edge_rows = jnp.concatenate([high, live_fill, middle, filler, low, filler], axis=1)
    group = 16
    dense = pl.pallas_call(
        spread_edges,
        grid=(node_count // group,),
        in_specs=[
            pl.BlockSpec((group, fanout), lambda i: (i, 0)),
            pl.BlockSpec((group, 24, fanout), lambda i: (i, 0, 0)),
        ],
        out_specs=pl.BlockSpec((group, 8, slot_count), lambda i: (i, 0, 0)),
        out_shape=jax.ShapeDtypeStruct((node_count, 8, slot_count), jnp.float32),
        cost_estimate=pl.CostEstimate(
            flops=2 * node_count * 24 * fanout * slot_count,
            bytes_accessed=32 * node_count * slot_count,
            transcendentals=0,
        ),
    )(neighbours, edge_rows.astype(jnp.bfloat16))
    dense = jnp.transpose(dense, (1, 0, 2))
    mesh_wide, mesh_factor, mesh_normed = normalize(mesh_h, gain_mesh)
    queries = (
        jnp.dot(mesh_normed, w_query, preferred_element_type=jnp.float32) * logit_scale
    ).astype(jnp.bfloat16)
    att_grad = jnp.einsum("me,de->md", out_grad, w_out, preferred_element_type=jnp.float32).astype(
        jnp.bfloat16
    )
    by_head = pl.BlockSpec((node_count, head_width), lambda h: (0, h))
    attended_rows, query_gradient, back = pl.pallas_call(
        functools.partial(attend, logit_scale),
        grid=(head_count,),
        in_specs=[
            by_head,
            pl.BlockSpec((slot_count, head_width), lambda h: (0, h)),
            pl.BlockSpec((slot_count, head_width), lambda h: (0, head_count + h)),
            by_head,
            pl.BlockSpec((1, node_count, slot_count), lambda h: (h, 0, 0)),
            pl.BlockSpec((1, node_count, slot_count), lambda h: (head_count, 0, 0)),
        ],
        out_specs=[
            by_head,
            by_head,
            pl.BlockSpec((2, slot_count, head_width), lambda h: (0, 0, h)),
        ],
        out_shape=[
            jax.ShapeDtypeStruct((node_count, model_width), jnp.bfloat16),
            jax.ShapeDtypeStruct((node_count, model_width), jnp.bfloat16),
            jax.ShapeDtypeStruct((2, slot_count, model_width), jnp.bfloat16),
        ],
        cost_estimate=pl.CostEstimate(
            flops=12 * node_count * slot_count * model_width,
            bytes_accessed=8 * slot_count * model_width,
            transcendentals=node_count * head_count * slot_count,
        ),
    )(queries, recv_pair, recv_pair, att_grad, dense, dense)
    mesh_out = (
        mesh_wide + jnp.dot(attended_rows, w_out, preferred_element_type=jnp.float32)
    ).astype(jnp.bfloat16)
    grad_wo = jnp.einsum("md,me->de", attended_rows, out_grad, preferred_element_type=jnp.float32)
    grad_wk = jnp.einsum("sd,se->de", arrived, back[0], preferred_element_type=jnp.float32)
    grad_wv = jnp.einsum("sd,se->de", arrived, back[1], preferred_element_type=jnp.float32)
    grad_wq = jnp.einsum(
        "md,me->de", mesh_normed, query_gradient, preferred_element_type=jnp.float32
    )
    weight_grads = reduce_weights(jnp.stack([grad_wq, grad_wk, grad_wv, grad_wo]))
    back_packet = (
        jnp.concatenate([back[0], back[1]], axis=1)
        .reshape(3, block, 2 * model_width)
    )
    home_pieces = []
    for offset in (0, 1, 2):
        piece = back_packet[offset]
        if offset != 1:
            piece = from_behind(piece, "grid", 1 - offset)
        home_pieces.append(piece)
    home = jnp.stack(home_pieces)
    home = home.reshape(3, sub_count, slots_per, 2 * model_width)
    returned = lax.all_to_all(home, "sub", split_axis=1, concat_axis=1, tiled=True).reshape(
        slot_count, 2 * model_width
    )
    slot_back = jnp.einsum("se,de->sd", returned, w_pair, preferred_element_type=jnp.float32)
    normed_grad = jnp.einsum(
        "sp,sd->pd",
        send_onehot,
        slot_back.astype(jnp.bfloat16),
        preferred_element_type=jnp.float32,
    )
    grid_grad = normalize_back(grid_wide, grid_factor, gain_grid, normed_grad).astype(jnp.bfloat16)
    mesh_normed_grad = jnp.einsum(
        "me,de->md", query_gradient, w_query, preferred_element_type=jnp.float32
    )
    mesh_grad = (
        out_grad.astype(jnp.float32)
        + normalize_back(mesh_wide, mesh_factor, gain_mesh, mesh_normed_grad)
    ).astype(jnp.bfloat16)
    return (mesh_out, mesh_grad, grid_grad, weight_grads)


def solution(mesh):
    in_specs = (
        P(("grid", "sub"), None),
        P(("grid", "sub"), None),
        P(),
        P(),
        P(),
        P(),
        P(),
        P(),
        P(("grid", "sub"), None),
        P(("grid", "sub"), None),
        P(("grid", "sub"), None),
        P(("grid", "sub"), None, None, None),
        P(("grid", "sub"), None),
    )
    out_specs = (P(("grid", "sub"), None), P(("grid", "sub"), None), P(("grid", "sub"), None), P())
    return jax.shard_map(shards, mesh=mesh, in_specs=in_specs, out_specs=out_specs, check_vma=False)
```

time: 304 us -> 269 us (0.88)
  matrix products: 49.8 us -> 19.5 us
  waiting for transfers between devices: 184 us -> 155 us
  Pallas kernels: 0 us -> 12.9 us
  local copies, waits for them, and re-layouts: 25.1 us -> 32.8 us
  other arithmetic: 8.64 us -> 13.7 us
    dot_general x12 -> x3, matrix products: 42.2 us -> 9.97 us  [the longest x1 6.88 us: shards(): jnp.einsum('sp,sd->pd', send_onehot, slot_back.astype(jnp.bfloat16), pref...]
    psum x1, waiting for transfers between devices: 138 us -> 117 us  [reduce_weights(): return lax.psum(local_grads, ('grid', 'sub'))]
    pallas_call x0 -> x2, Pallas kernels: none -> 12.9 us  [the longest x1 6.45 us: shards(): pl.pallas_call(functools.partial(attend, logit_scale), grid=(head_count,)...]
    all_to_all x1, waiting for transfers between devices: 17 us -> 4.96 us  [shards(): lax.all_to_all(packet, 'sub', split_axis=1, concat_axis=1, tiled=True)]
    all_to_all x1, waiting for transfers between devices: 24.3 us -> 31.5 us  [shards(): lax.all_to_all(home, 'sub', split_axis=1, concat_axis=1, tiled=True)]
    unnamed x69 -> x40, local copies, waits for them, and re-layouts: 19.4 us -> 14 us
    concatenate x0 -> x1, local copies, waits for them, and re-layouts: none -> 4.87 us  [shards(): jnp.concatenate([high, live_fill, middle, filler, low, filler], axis=1)]
    pallas_call x0 -> x1, local copies, waits for them, and re-layouts: none -> 3.16 us  [shards(): pl.pallas_call(spread_edges, grid=(node_count // group,), in_specs=[pl.Bl...]
  transfers between devices with their start and end apart: 7 -> 7, of which waited for: 5 -> 4; matrix products, arithmetic and copies ran while one was open for 10% -> 17% of each run, Pallas kernels for 0% -> 2%
where the time goes in v1:
time: 269 us; the launch traced here: 268 us
  waiting for transfers between devices  155 us (58%)
  local copies, waits for them, and re-layouts  32.8 us (12%)
  starting transfers between devices  20.4 us (8%)
  matrix products  19.5 us (7%)
  between operations  14.3 us (5%)
  other arithmetic  13.7 us (5%)
  Pallas kernels  12.9 us (5%)
    psum x1, waiting for transfers between devices, reduce_weights(): return lax.psum(local_grads, ('grid', 'sub'))  117 us
    all_to_all x1, waiting for transfers between devices, shards(): lax.all_to_all(home, 'sub', split_axis=1, concat_axis=1, tiled=True)  31.5 us
    unnamed x40, local copies, waits for them, and re-layouts  14 us
    ppermute x4, starting transfers between devices, from_behind(): return lax.ppermute(block, axis, route)  9.29 us
    dot_general x1, matrix products, shards(): jnp.einsum('sp,sd->pd', send_onehot, slot_back.astype(jnp.bfloat16), pref...  6.88 us
    pallas_call x1, Pallas kernels, shards(): pl.pallas_call(functools.partial(attend, logit_scale), grid=(head_count,)...  6.45 us
    pallas_call x1, Pallas kernels, shards(): pl.pallas_call(spread_edges, grid=(node_count // group,), in_specs=[pl.Bl...  6.44 us
    all_to_all x1, starting transfers between devices, shards(): lax.all_to_all(packet, 'sub', split_axis=1, concat_axis=1, tiled=True)  6.35 us
  transfers between devices with their start and end apart: 7, of which 4 were waited for; matrix products, arithmetic and copies ran while one was open for 17% of the time, Pallas kernels for 2%

profile of v1, /device:TPU:0, one launch (start us, length us, event | category | flops | bytes accessed | tf_op | source)
XLA Modules:
  0.0 268.1 jit_solution(15670856888362652112)
XLA Ops:
  7.2 3.0 %copy.32 = bf16[2048,512]{0,1:T(8,128)(2,1)S(1)} copy(bf16[2048,512]{1,0:T(8,128)(2,1)} %param.13) | data formatting | bytes 4194304 | tf_op args[0]
  11.0 2.0 fusion.14
  13.9 6.3 %all-to-all-start = ((bf16[3,4,64,512]{3,2,0,1:T(8,128)(2,1)}), bf16[3,4,64,512]{3,2,0,1:T(8,128)(2,1)S(1)}, u32[]{:S(2)}, u32[]{:S(2)}) async-start(bf16[3,4,64,512]{3,2,0,1:T(8,128)(2,1)} %copy.33), calls=%async_computation | async-start | bytes 1572864 | tf_op jit(solution)/shard_map/all_to_all | solution.py:108
  20.2 1.7 reshape.77
  23.3 1.7 fusion.21
  26.2 4.9 %concatenate.16.rows_ref = bf16[64,24,96]{2,1,0:T(8,128)(2,1)} concatenate(bf16[64,4,96]{2,1,0:T(4,128)(2,1)} %get-tuple-element.36, bf16[64,1,96]{2,1,0:T(2,128)(2,1)} %copy.34, bf16[64,3,96]{2,1,0:T(4,128)(2,1)} %slice.38, bf16[64,4,96]{2,1,0:T(4,128)(2,1)} %get-tuple-element.35, bf16[64,4,96]{2,1,0:T(4,128)(2,1)} %broadcast_in_dim.9, bf16[64,4,96]{2,1,0:T(4,128)(2,1)} %get-tuple-element.34, ...), dimensions={1} | concatenate | bytes 589824 | tf_op jit(solution)/shard_map/concatenate | solution.py:126
  35.4 5.0 %all-to-all-done = bf16[3,4,64,512]{3,2,0,1:T(8,128)(2,1)S(1)} async-done(((bf16[3,4,64,512]{3,2,0,1:T(8,128)(2,1)}), bf16[3,4,64,512]{3,2,0,1:T(8,128)(2,1)S(1)}, u32[]{:S(2)}, u32[]{:S(2)}) %all-to-all-start) | async-done | bytes 786464 | tf_op jit(solution)/shard_map/all_to_all | solution.py:108
  43.9 6.4 %shard_map.156 = f32[64,8,768]{2,1,0:T(8,128)} custom-call(s32[64,96]{1,0:T(8,128)} %nbr_ref.1, bf16[64,24,96]{2,1,0:T(8,128)(2,1)} %concatenate.16.rows_ref), custom_call_target="tpu_custom_call" | custom-call | flops 226492416 | bytes 1572864 | tf_op jit(solution)/shard_map/pallas_call | solution.py:128
  50.3 3.2 %copy.42 = f32[64,8,768]{2,0,1:T(8,128)} copy(f32[64,8,768]{2,1,0:T(8,128)} %shard_map.156) | data formatting | bytes 3145728 | tf_op jit(solution)/shard_map/pallas_call | solution.py:128
  54.4 3.1 %convolution_convert_fusion.k_ref.v_ref = bf16[768,1024]{1,0:T(8,128)(2,1)} fusion(bf16[512,1024]{1,0:T(8,128)(2,1)S(1)} %copy-done.7, bf16[256,512]{1,0:T(8,128)(2,1)S(1)} %collective-permute-done.1, bf16[256,512]{1,0:T(8,128)(2,1)S(1)} %bitcast.53, bf16[256,512]{1,0:T(8,128)(2,1)} %collective-permute-done), kind=kOutput, calls=%fused_computation.23 | convolution fusion | flops 808452096 | bytes 3407872 | tf_op jit(solution)/shard_map/dot_general | solution.py:118
  57.5 6.5 %shard_map.157 = (bf16[64,512]{1,0:T(8,128)(2,1)}, bf16[64,512]{1,0:T(8,128)(2,1)}, bf16[2,768,512]{2,1,0:T(8,128)(2,1)}) custom-call(bf16[64,512]{1,0:T(8,128)(2,1)} %fusion.17.q_ref, bf16[768,1024]{1,0:T(8,128)(2,1)} %convolution_convert_fusion.k_ref.v_ref, bf16[768,1024]{1,0:T(8,128)(2,1)} %convolution_convert_fusion.k_ref.v_ref, ...), custom_call_target="tpu_custom_call" | custom-call | flops 301989888 | bytes 3145728 | tf_op jit(solution)/shard_map/pallas_call | solution.py:152
  66.9 5.4 %collective-permute-start.2 = (bf16[256,1024]{1,0:T(8,128)(2,1)S(1)}, bf16[256,1024]{1,0:T(8,128)(2,1)S(1)}, u32[]{:S(2)}, u32[]{:S(2)}) collective-permute-start(bf16[256,1024]{1,0:T(8,128)(2,1)S(1)} %get-tuple-element.26), channel_id=1, source_target_pairs={{0,4},{4,8},{8,12},{12,16},{16,20},{20,24},{24,28},{1,5},{5,9},{9,... | collective-permute-start | bytes 1572872 | tf_op jit(solution)/shard_map/ppermute | solution.py:16
  72.3 1.5 collective-permute-done.2
  75.1 4.5 %all-to-all-start.1 = ((bf16[3,4,64,1024]{3,2,0,1:T(8,128)(2,1)}), bf16[3,4,64,1024]{3,2,0,1:T(8,128)(2,1)}, u32[]{:S(2)}, u32[]{:S(2)}) async-start(bf16[3,4,64,1024]{3,2,0,1:T(8,128)(2,1)} %pad_maximum_fusion.1), calls=%async_computation.1 | async-start | bytes 3145728 | tf_op jit(solution)/shard_map/all_to_all | solution.py:201
  81.3 1.5 convolution_bitcast_fusion.2
  82.8 1.5 convolution_bitcast_fusion.3
  84.4 2.4 pad_maximum_fusion
  90.3 31.5 %all-to-all-done.1 = bf16[3,4,64,1024]{3,2,0,1:T(8,128)(2,1)} async-done(((bf16[3,4,64,1024]{3,2,0,1:T(8,128)(2,1)}), bf16[3,4,64,1024]{3,2,0,1:T(8,128)(2,1)}, u32[]{:S(2)}, u32[]{:S(2)}) %all-to-all-start.1) | async-done | bytes 1572896 | tf_op jit(solution)/shard_map/all_to_all | solution.py:201
  121.7 2.7 %copy.39 = bf16[3,4,64,1024]{3,2,1,0:T(8,128)(2,1)} copy(bf16[3,4,64,1024]{3,2,0,1:T(8,128)(2,1)} %all-to-all-done.1) | data formatting | bytes 3145728 | tf_op jit(solution)/shard_map/all_to_all | solution.py:201
  124.4 6.9 %fusion.8 = (f32[2048]{0:T(1024)S(1)}, f32[2048,512]{0,1:T(8,128)}) fusion(bf16[2048,512]{0,1:T(8,128)(2,1)S(1)} %copy.32, f32[512]{0:T(512)S(1)} %copy-done.17, bf16[768,1024]{1,0:T(8,128)(2,1)} %bitcast.49, bf16[512,1024]{1,0:T(8,128)(2,1)} %copy-done.6, s32[768]{0:T(1024)S(1)} %copy-done.15), kind=kOutput, calls=%fused_computation.13 | convolution fusion | flops 2422077440 | bytes 8926208 | tf_op jit(solution)/shard_map/sp,sd->pd/dot_general | solution.py:205
  131.3 4.7 %fusion.7 = bf16[2048,512]{0,1:T(8,128)(2,1)} fusion(bf16[2048,512]{0,1:T(8,128)(2,1)S(1)} %copy.32, f32[2048,512]{0,1:T(8,128)} %get-tuple-element.44, f32[2048]{0:T(1024)S(1)} %broadcast_multiply_fusion, f32[2048]{0:T(1024)S(1)} %get-tuple-element.37, f32[512]{0:T(512)S(1)} %copy-done.17, f32[2048]{0:T(1024)S(1)} %get-tuple-element.38), kind=kLoop, calls=%fused_computation.12 | loop fusion | flops 7340032 | bytes 8415232 | tf_op jit(solution)/shard_map/convert_element_type | solution.py:211
  136.0 4.0 %copy.40 = bf16[2048,512]{1,0:T(8,128)(2,1)} copy(bf16[2048,512]{0,1:T(8,128)(2,1)} %fusion.7) | data formatting | bytes 4194304
  140.0 116.6 %all-reduce.2.cloned.1.call-done = f32[4,512,512]{2,1,0:T(8,128)} async-done(((f32[4,512,512]{2,1,0:T(8,128)}), f32[4,512,512]{2,1,0:T(8,128)}) %all-reduce.2.cloned.1.call-update) | async-done | bytes 4194320 | tf_op jit(solution)/shard_map/psum | solution.py:70
  256.6 4.6 %copy.45 = f32[4,512,512]{2,1,0:T(8,128)} copy(f32[4,512,512]{2,1,0:T(8,128)} %all-reduce.2.cloned.1.call-done) | data formatting | bytes 8388608
  (69 shorter events, 22.3 us)
Async XLA Ops:
  7.2 46.3 %copy-start = (bf16[512,512]{1,0:T(8,128)(2,1)S(1)}, bf16[512,512]{1,0:T(8,128)(2,1)}, u32[]{:S(2)}) copy-start(bf16[512,512]{1,0:T(8,128)(2,1)} %param.17) | copy-start | bytes 1572868
  10.2 0.8 copy-start.16
  10.9 2.0 copy-start.14
  12.9 18.2 %copy-start.1 = (bf16[64,512]{1,0:T(8,128)(2,1)S(1)}, bf16[64,512]{1,0:T(8,128)(2,1)}, u32[]{:S(2)}) copy-start(bf16[64,512]{1,0:T(8,128)(2,1)} %param.14) | copy-start | bytes 196612
  13.9 26.5 %all-to-all-start = ((bf16[3,4,64,512]{3,2,0,1:T(8,128)(2,1)}), bf16[3,4,64,512]{3,2,0,1:T(8,128)(2,1)S(1)}, u32[]{:S(2)}, u32[]{:S(2)}) async-start(bf16[3,4,64,512]{3,2,0,1:T(8,128)(2,1)} %copy.33), calls=%async_computation | async-start | bytes 1572864 | tf_op jit(solution)/shard_map/all_to_all | solution.py:108
  20.2 14.2 %copy-start.5 = (bf16[64,512]{1,0:T(8,128)(2,1)S(1)}, bf16[64,512]{1,0:T(8,128)(2,1)}, u32[]{:S(2)}) copy-start(bf16[64,512]{1,0:T(8,128)(2,1)} %param.25) | copy-start | bytes 196612
  31.1 3.3 %copy-start.2 = (bf16[512,512]{1,0:T(8,128)(2,1)S(1)}, bf16[512,512]{1,0:T(8,128)(2,1)}, u32[]{:S(2)}) copy-start(bf16[512,512]{1,0:T(8,128)(2,1)} %param.20) | copy-start | bytes 1572868
  33.5 1.0 copy-start.6
  41.2 13.1 %collective-permute-start.1 = (bf16[256,512]{1,0:T(8,128)(2,1)}, bf16[256,512]{1,0:T(8,128)(2,1)S(1)}, u32[]{:S(2)}, u32[]{:S(2)}) collective-permute-start(bf16[256,512]{1,0:T(8,128)(2,1)} %bitcast.3), channel_id=1, source_target_pairs={{0,4},{4,8},{8,12},{12,16},{16,20},{20,24},{24,28},{1,5},{5,9},{9,... | collective-permute-start | bytes 786440 | tf_op jit(solution)/shard_map/ppermute | solution.py:16
  42.5 10.9 %copy-start.11 = (f32[512]{0:T(512)S(1)}, f32[512]{0:T(512)}, u32[]{:S(2)}) copy-start(f32[512]{0:T(512)} %param.16) | copy-start | bytes 6148
  42.5 10.9 %copy-start.13 = (f32[64]{0:T(128)S(1)}, f32[64]{0:T(128)}, u32[]{:S(2)}) copy-start(f32[64]{0:T(128)} %get-tuple-element.40) | copy-start | bytes 772
  42.6 11.8 %collective-permute-start = (bf16[256,512]{1,0:T(8,128)(2,1)}, bf16[256,512]{1,0:T(8,128)(2,1)}, u32[]{:S(2)}, u32[]{:S(2)}) collective-permute-start(bf16[256,512]{1,0:T(8,128)(2,1)} %bitcast.1), channel_id=1, source_target_pairs={{4,0},{8,4},{12,8},{16,12},{20,16},{24,20},{28,24},{5,1},{9,5},{13... | collective-permute-start | bytes 786440 | tf_op jit(solution)/shard_map/ppermute | solution.py:16
  50.3 4.1 %copy-start.7 = (bf16[512,1024]{1,0:T(8,128)(2,1)S(1)}, bf16[512,1024]{1,0:T(8,128)(2,1)}, u32[]{:S(2)}) copy-start(bf16[512,1024]{1,0:T(8,128)(2,1)} %copy-done.6) | copy-start | bytes 3145732
  50.3 4.1 %copy-start.8 = (bf16[1,4,64,512]{3,2,0,1:T(8,128)(2,1)S(1)}, bf16[1,4,64,512]{3,2,0,1:T(8,128)(2,1)}, u32[]{:S(2)}) copy-start(bf16[1,4,64,512]{3,2,0,1:T(8,128)(2,1)} %get-tuple-element.33) | copy-start | bytes 786436
  65.6 6.7 %collective-permute-start.3 = (bf16[256,1024]{1,0:T(8,128)(2,1)S(1)}, bf16[256,1024]{1,0:T(8,128)(2,1)S(1)}, u32[]{:S(2)}, u32[]{:S(2)}) collective-permute-start(bf16[256,1024]{1,0:T(8,128)(2,1)S(1)} %get-tuple-element.27), channel_id=1, source_target_pairs={{4,0},{8,4},{12,8},{16,12},{20,16},{24,20},{28,24},{5,1},{9,5},{13... | collective-permute-start | bytes 1572872 | tf_op jit(solution)/shard_map/ppermute | solution.py:16
  66.9 6.9 %collective-permute-start.2 = (bf16[256,1024]{1,0:T(8,128)(2,1)S(1)}, bf16[256,1024]{1,0:T(8,128)(2,1)S(1)}, u32[]{:S(2)}, u32[]{:S(2)}) collective-permute-start(bf16[256,1024]{1,0:T(8,128)(2,1)S(1)} %get-tuple-element.26), channel_id=1, source_target_pairs={{0,4},{4,8},{8,12},{12,16},{16,20},{20,24},{24,28},{1,5},{5,9},{9,... | collective-permute-start | bytes 1572872 | tf_op jit(solution)/shard_map/ppermute | solution.py:16
  75.1 4.8 %copy-start.9 = (bf16[64,512]{1,0:T(8,128)(2,1)S(1)}, bf16[64,512]{1,0:T(8,128)(2,1)}, u32[]{:S(2)}) copy-start(bf16[64,512]{1,0:T(8,128)(2,1)} %get-tuple-element.7) | copy-start | bytes 196612
  75.1 5.1 %copy-start.10 = (bf16[64,512]{1,0:T(8,128)(2,1)S(1)}, bf16[64,512]{1,0:T(8,128)(2,1)}, u32[]{:S(2)}) copy-start(bf16[64,512]{1,0:T(8,128)(2,1)} %get-tuple-element.8) | copy-start | bytes 196612
  75.1 46.6 %all-to-all-start.1 = ((bf16[3,4,64,1024]{3,2,0,1:T(8,128)(2,1)}), bf16[3,4,64,1024]{3,2,0,1:T(8,128)(2,1)}, u32[]{:S(2)}, u32[]{:S(2)}) async-start(bf16[3,4,64,1024]{3,2,0,1:T(8,128)(2,1)} %pad_maximum_fusion.1), calls=%async_computation.1 | async-start | bytes 3145728 | tf_op jit(solution)/shard_map/all_to_all | solution.py:201
  79.6 176.9 %all-reduce.2.cloned.1.call-start = ((), (), s32[]{:S(2)}) async-start(), calls=%async_computation.2 | async-start | bytes 8388608 | tf_op jit(solution)/shard_map/psum | solution.py:70
  79.9 1.4 copy-start.4
  86.8 2.6 copy-start.3
  88.0 36.4 %copy-start.15 = (s32[768]{0:T(1024)S(1)}, s32[768]{0:T(1024)}, u32[]{:S(2)}) copy-start(s32[768]{0:T(1024)} %copy-done.14) | copy-start | bytes 9220
  88.0 36.4 %copy-start.17 = (f32[512]{0:T(512)S(1)}, f32[512]{0:T(512)}, u32[]{:S(2)}) copy-start(f32[512]{0:T(512)} %param.15) | copy-start | bytes 6148
  (1 other events, 0.7 us)
Sparse Core Ops, SparseCore 0:
  87.0 169.5 all-reduce.1
